TPU v7x, 32 devices: a whole 2x2x4 slice. The times are simulated.
32 devices in a mesh: section: 8 (over z, core), tensor: 2 (over x), replica: 2 (over y).
Axes of the slice: x: 2, y: 2, z: 4, core: 2. Of those that a mesh axis runs over, the one named last changes fastest.
Arguments:
- pool_inputs: bfloat16 [8, 256, 2, 1408], P('section', 'replica', None, 'tensor'), may hold values from -6 to 6
- pool_mixed: bfloat16 [8, 256, 1408], P('section', 'replica'), may hold values from -6 to 6
- crop_ids: int32 [8, 8, 128], P('section', 'replica'), may hold values from 0 to 127
- incoming: bfloat16 [8, 256, 1408], P('section', 'replica', 'tensor'), may hold values from -6 to 6
- loss_grads: bfloat16 [3, 256, 1408], P(None, 'replica', 'tensor'), may hold values from -6 to 6
- w_proj: bfloat16 [8, 2, 1408, 1408], P('section', None, ('tensor', 'replica')), may hold values from -0.109375 to 0.109375
- w_up: bfloat16 [8, 1408, 3072], P('section', None, ('tensor', 'replica')), may hold values from -0.15625 to 0.15625
- w_down: bfloat16 [8, 3072, 1408], P('section', ('tensor', 'replica')), may hold values from -0.109375 to 0.109375
Outputs:
- grad_proj: bfloat16 [8, 2, 1408, 1408], P('section', None, ('tensor', 'replica'))
- grad_up: bfloat16 [8, 1408, 3072], P('section', None, ('tensor', 'replica'))
- grad_down: bfloat16 [8, 3072, 1408], P('section', ('tensor', 'replica'))
- outgoing: bfloat16 [8, 256, 2, 1408], P('section', 'replica', None, 'tensor')
All inputs are finite; a program needn't handle non-finite values.
Results may differ from a plain program's by a relative error of at most 0.02.
Values may be sent and summed in bfloat16 or wider, within the bound.
A program may use at most 128 MiB of HBM per device.

v0:
```python
import jax
import jax.numpy as jnp
from jax import lax
from jax.sharding import PartitionSpec as P

gelu_scale = 0.7978845608
gelu_cubic = 0.044715


def from_partner(value, axis, bit):
    mask = 2**bit
    pairs = [(source, source ^ mask) for source in range(lax.axis_size(axis))]
    return lax.ppermute(value, axis, pairs)


def shifted(x, axis, by):
    devices = lax.axis_size(axis)
    pairs = [(i, i + by) for i in range(devices) if 0 <= i + by < devices]
    return lax.ppermute(x, axis, pairs)


def gelu_pair(pre_gelu):
    inner = gelu_scale * (pre_gelu + gelu_cubic * pre_gelu * pre_gelu * pre_gelu)
    tanh_part = jnp.tanh(inner)
    gelu_value = 0.5 * pre_gelu * (1.0 + tanh_part)
    gelu_slope = 0.5 * (1.0 + tanh_part) + 0.5 * pre_gelu * (
        1.0 - tanh_part * tanh_part
    ) * gelu_scale * (1.0 + 3.0 * gelu_cubic * pre_gelu * pre_gelu)
    return (gelu_value, gelu_slope)


def reflect(block, section_count):
    for bit_number in range(section_count.bit_length() - 1):
        block = from_partner(block, "section", bit_number)
    return block


def body(pool_inputs, pool_mixed, crop_ids, incoming, loss_grads, w_proj, w_up, w_down):
    section_index = lax.axis_index("section")
    section_count = lax.axis_size("section")
    proj_full, up_full, down_full = (
        lax.all_gather(w_proj, "replica", axis=2, tiled=True),
        lax.all_gather(w_up, "replica", axis=2, tiled=True),
        lax.all_gather(w_down, "replica", axis=1, tiled=True),
    )
    proj_local = proj_full[0]
    up_local = up_full[0]
    down_local = down_full[0]
    seed_full, loss_full = (
        lax.all_gather(incoming, "tensor", axis=2, tiled=True),
        lax.all_gather(loss_grads, "tensor", axis=2, tiled=True),
    )
    encoder = section_index < section_count // 2
    decoder_flag = jnp.where(encoder, 0.0, 1.0).astype(jnp.bfloat16)
    skip_mask = jnp.stack([jnp.ones((), jnp.bfloat16), decoder_flag])[None, :, None]
    encoder_weight = jnp.where(encoder, 1.0, 0.0).astype(jnp.float32)
    is_top = section_index == section_count - 1
    tick_count = crop_ids.shape[1]
    upstream = seed_full[0]
    kept_inputs, kept_mixed, kept_active, kept_hidden, kept_grads, kept_upstream = (
        [],
        [],
        [],
        [],
        [],
        [],
    )
    input_grad = None
    for tick_index in range(tick_count):
        picked_rows = crop_ids[0, tick_index]
        inputs = pool_inputs[0][picked_rows] * skip_mask
        mixed_rows = pool_mixed[0][picked_rows]
        pre_gelu = jnp.dot(mixed_rows, up_local, preferred_element_type=jnp.float32)
        gelu_value, gelu_slope = gelu_pair(pre_gelu)
        activated = gelu_value.astype(jnp.bfloat16)
        back_act = jnp.einsum("md,fd->mf", upstream, down_local, preferred_element_type=jnp.float32)
        back_hidden = (back_act * gelu_slope).astype(jnp.bfloat16)
        partial_back = jnp.einsum(
            "mf,df->md", back_hidden, up_local, preferred_element_type=jnp.float32
        )
        back_mixed = upstream.astype(jnp.float32) + lax.psum(partial_back, "tensor")
        mixed_grad = back_mixed.astype(jnp.bfloat16)
        input_grad = jnp.einsum(
            "mj,kij->mki", mixed_grad, proj_local, preferred_element_type=jnp.float32
        ).astype(jnp.bfloat16)
        kept_inputs.append(inputs)
        kept_mixed.append(mixed_rows)
        kept_active.append(activated)
        kept_hidden.append(back_hidden)
        kept_grads.append(mixed_grad)
        kept_upstream.append(upstream)
        if tick_index + 1 < tick_count:
            from_above = shifted(input_grad[:, 0], "section", -1)
            mirrored = reflect(input_grad[:, 1], section_count)
            summed = (
                from_above.astype(jnp.float32) + encoder_weight * mirrored.astype(jnp.float32)
            ).astype(jnp.bfloat16)
            summed = lax.all_gather(summed, "tensor", axis=1, tiled=True)
            upstream = jnp.where(is_top, loss_full[tick_index], summed)
    all_inputs = jnp.concatenate(kept_inputs, axis=0)
    all_mixed = jnp.concatenate(kept_mixed, axis=0)
    all_active = jnp.concatenate(kept_active, axis=0)
    all_hidden = jnp.concatenate(kept_hidden, axis=0)
    all_grads = jnp.concatenate(kept_grads, axis=0)
    all_upstream = jnp.concatenate(kept_upstream, axis=0)
    down_total = jnp.einsum(
        "mf,md->fd", all_active, all_upstream, preferred_element_type=jnp.float32
    )
    up_total = jnp.einsum("md,mf->df", all_mixed, all_hidden, preferred_element_type=jnp.float32)
    proj_total = jnp.einsum(
        "mki,mj->kij", all_inputs, all_grads, preferred_element_type=jnp.float32
    )
    reduced = (
        lax.psum_scatter(
            proj_total[None].astype(jnp.bfloat16), "replica", scatter_dimension=2, tiled=True
        ).astype(jnp.float32),
        lax.psum_scatter(
            up_total[None].astype(jnp.bfloat16), "replica", scatter_dimension=2, tiled=True
        ).astype(jnp.float32),
        lax.psum_scatter(
            down_total[None].astype(jnp.bfloat16), "replica", scatter_dimension=1, tiled=True
        ).astype(jnp.float32),
    )
    return (
        reduced[0].astype(jnp.bfloat16),
        reduced[1].astype(jnp.bfloat16),
        reduced[2].astype(jnp.bfloat16),
        input_grad[None],
    )


def solution(mesh):
    in_specs = (
        P("section", "replica", None, "tensor"),
        P("section", "replica", None),
        P("section", "replica", None),
        P("section", "replica", "tensor"),
        P(None, "replica", "tensor"),
        P("section", None, ("tensor", "replica"), None),
        P("section", None, ("tensor", "replica")),
        P("section", ("tensor", "replica"), None),
    )
    out_specs = (
        P("section", None, ("tensor", "replica"), None),
        P("section", None, ("tensor", "replica")),
        P("section", ("tensor", "replica"), None),
        P("section", "replica", None, "tensor"),
    )
    return jax.shard_map(body, mesh=mesh, in_specs=in_specs, out_specs=out_specs, check_vma=False)
```

profile of v0, /device:TPU:0, one launch (start us, length us, event | category | flops | bytes accessed | tf_op | source)
XLA Modules:
  0.0 637.9 jit_solution(14734872152342492354)
XLA Ops:
  9.7 8.2 %all_gather.24 = bf16[1,128,1408]{1,2,0:T(8,128)(2,1)S(1)} all-gather(bf16[1,128,704]{1,2,0:T(8,128)(2,1)S(1)} %copy-done.23), channel_id=1, replica_groups=mesh['section'=8,'tensor'=2,'replica'=2] {'tensor'}, dimensions={2}, use_global_device_ids=true | all-gather | bytes 540672 | tf_op jit(solution)/shard_map/all_gather | solution.py:50
  17.9 52.6 %all-gather.7.cloned.1.call-done = bf16[1,1408,1536]{2,1,0:T(8,128)(2,1)} async-done(((bf16[1,1408,768]{2,1,0:T(8,128)(2,1)}), bf16[1,1408,1536]{2,1,0:T(8,128)(2,1)}) %all-gather.7.cloned.1.call-update) | async-done | bytes 4325392 | tf_op jit(solution)/shard_map/all_gather | solution.py:43
  70.5 4.0 multiply_convert_fusion.3
  74.5 55.8 %all-gather.5.cloned.1.call-done = bf16[1,1536,1408]{2,1,0:T(8,128)(2,1)} async-done(((bf16[1,768,1408]{2,1,0:T(8,128)(2,1)}), bf16[1,1536,1408]{2,1,0:T(8,128)(2,1)}) %all-gather.5.cloned.1.call-update) | async-done | bytes 4325392 | tf_op jit(solution)/shard_map/all_gather | solution.py:44
  130.3 4.0 fusion.56
  138.9 31.7 %all-reduce.5.cloned.1.call-done = f32[128,1408]{1,0:T(8,128)} async-done(((f32[128,1408]{1,0:T(8,128)}), f32[128,1408]{1,0:T(8,128)}) %all-reduce.5.cloned.1.call-update) | async-done | bytes 720912 | tf_op jit(solution)/shard_map/psum | solution.py:81
  171.7 54.4 %all-gather.11.cloned.1.call-done = bf16[1,2,704,1408]{3,2,1,0:T(8,128)(2,1)} async-done(((bf16[1,2,352,1408]{3,2,1,0:T(8,128)(2,1)}), bf16[1,2,704,1408]{3,2,1,0:T(8,128)(2,1)}) %all-gather.11.cloned.1.call-update) | async-done | bytes 3964944 | tf_op jit(solution)/shard_map/all_gather | solution.py:42
  232.4 16.7 %all-gather.9.cloned.1.call-done = bf16[3,128,1408]{1,2,0:T(8,128)(2,1)} async-done(((bf16[3,128,704]{1,2,0:T(8,128)(2,1)}), bf16[3,128,1408]{1,2,0:T(8,128)(2,1)}) %all-gather.9.cloned.1.call-update) | async-done | bytes 1081360 | tf_op jit(solution)/shard_map/all_gather | solution.py:51
  255.1 4.2 multiply_convert_fusion.2
  259.2 6.9 %collective-permute-done.3 = bf16[128,704]{0,1:T(8,128)(2,1)S(1)} collective-permute-done((bf16[128,704]{0,1:T(8,128)(2,1)S(1)}, bf16[128,704]{0,1:T(8,128)(2,1)S(1)}, u32[]{:S(2)}, u32[]{:S(2)}) %collective-permute-start.3) | collective-permute-done | bytes 180256 | tf_op jit(solution)/shard_map/ppermute | solution.py:13
  266.2 6.2 all_gather.29
  272.7 4.2 fusion.53
  280.1 32.3 %all-reduce.7.cloned.1.call-done = f32[128,1408]{1,0:T(8,128)} async-done(((f32[128,1408]{1,0:T(8,128)}), f32[128,1408]{1,0:T(8,128)}) %all-reduce.7.cloned.1.call-update) | async-done | bytes 720912 | tf_op jit(solution)/shard_map/psum | solution.py:81
  313.6 3.5 fusion.103
  327.6 4.1 multiply_convert_fusion.1
  331.7 5.0 collective-permute-done.7
  336.7 6.4 %all_gather.30 = bf16[128,1408]{0,1:T(8,128)(2,1)S(1)} all-gather(bf16[128,704]{0,1:T(8,128)(2,1)S(1)} %add_convert_fusion.5), channel_id=1, replica_groups=mesh['section'=8,'tensor'=2,'replica'=2] {'tensor'}, dimensions={1}, use_global_device_ids=true | all-gather | bytes 540672 | tf_op jit(solution)/shard_map/all_gather | solution.py:98
  343.4 4.2 fusion.50
  350.9 32.9 %all-reduce.9.cloned.1.call-done = f32[128,1408]{1,0:T(8,128)} async-done(((f32[128,1408]{1,0:T(8,128)}), f32[128,1408]{1,0:T(8,128)}) %all-reduce.9.cloned.1.call-update) | async-done | bytes 720912 | tf_op jit(solution)/shard_map/psum | solution.py:81
  385.0 3.4 fusion.106
  399.0 4.1 multiply_convert_fusion
  403.1 5.0 collective-permute-done.11
  408.2 6.2 all_gather.31
  414.6 4.2 fusion.47
  432.3 22.7 %all-reduce.11.cloned.1.call-done = f32[128,1408]{1,0:T(8,128)} async-done(((f32[128,1408]{1,0:T(8,128)}), f32[128,1408]{1,0:T(8,128)}) %all-reduce.11.cloned.1.call-update) | async-done | bytes 720912 | tf_op jit(solution)/shard_map/psum | solution.py:81
  456.3 5.7 fusion.34
  463.6 5.6 fusion
  470.8 4.6 fusion.1
  475.4 4.2 fusion.112
  479.6 34.5 %reduce-scatter.4.cloned.1.call-done = bf16[1,2,352,1408]{3,2,1,0:T(8,128)(2,1)} async-done(((bf16[1,2,704,1408]{3,2,1,0:T(8,128)(2,1)}), bf16[1,2,352,1408]{3,2,1,0:T(8,128)(2,1)}) %reduce-scatter.4.cloned.1.call-update) | async-done | bytes 1982480 | tf_op jit(solution)/shard_map/reduce_scatter | solution.py:114
  514.1 58.5 %reduce-scatter.6.cloned.1.call-done = bf16[1,1408,768]{2,1,0:T(8,128)(2,1)} async-done(((bf16[1,1408,1536]{2,1,0:T(8,128)(2,1)}), bf16[1,1408,768]{2,1,0:T(8,128)(2,1)}) %reduce-scatter.6.cloned.1.call-update) | async-done | bytes 2162704 | tf_op jit(solution)/shard_map/reduce_scatter | solution.py:117
  572.7 58.7 %reduce-scatter.8.cloned.1.call-done = bf16[1,768,1408]{2,1,0:T(8,128)(2,1)} async-done(((bf16[1,1536,1408]{2,1,0:T(8,128)(2,1)}), bf16[1,768,1408]{2,1,0:T(8,128)(2,1)}) %reduce-scatter.8.cloned.1.call-update) | async-done | bytes 2162704 | tf_op jit(solution)/shard_map/reduce_scatter | solution.py:120
  (167 shorter events, 68.6 us)
Async XLA Ops:
  7.2 63.3 %all-gather.7.cloned.1.call-start = ((), (), s32[]{:S(2)}) async-start(), calls=%async_computation.4 | async-start | bytes 6488064 | tf_op jit(solution)/shard_map/all_gather | solution.py:43
  7.9 122.3 %all-gather.5.cloned.1.call-start = ((), (), s32[]{:S(2)}) async-start(), calls=%async_computation.3 | async-start | bytes 6488064 | tf_op jit(solution)/shard_map/all_gather | solution.py:44
  8.7 161.8 %all-reduce.5.cloned.1.call-start = ((), (), s32[]{:S(2)}) async-start(), calls=%async_computation.5 | async-start | bytes 1441792 | tf_op jit(solution)/shard_map/psum | solution.py:81
  9.7 64.8 %copy-start.17 = (bf16[128,1408]{1,0:T(8,128)(2,1)}, bf16[128,1408]{1,0:T(8,128)(2,1)S(1)}, u32[]{:S(2)}) copy-start(bf16[128,1408]{1,0:T(8,128)(2,1)S(1)} %gather_fusion.4) | copy-start | bytes 1081348
  70.5 64.5 %slice-start = ((s8[4325376]{0:T(1024)(128)(4,1)}), s8[131072]{0:T(1024)(128)(4,1)S(1)}, s32[]{:S(2)}) async-start(s8[4325376]{0:T(1024)(128)(4,1)} %bitcast.149), calls=%async_computation.14 | async-start | bytes 262144
  137.4 88.7 %all-gather.11.cloned.1.call-start = ((), (), s32[]{:S(2)}) async-start(), calls=%async_computation.7 | async-start | bytes 5947392 | tf_op jit(solution)/shard_map/all_gather | solution.py:42
  138.0 111.2 %all-gather.9.cloned.1.call-start = ((), (), s32[]{:S(2)}) async-start(), calls=%async_computation.6 | async-start | bytes 1622016 | tf_op jit(solution)/shard_map/all_gather | solution.py:51
  138.6 173.8 %all-reduce.7.cloned.1.call-start = ((), (), s32[]{:S(2)}) async-start(), calls=%async_computation.8 | async-start | bytes 1441792 | tf_op jit(solution)/shard_map/psum | solution.py:81
  229.5 1.5 collective-permute-start.1
  230.5 28.8 %copy-start.19 = (bf16[128,1408]{1,0:T(8,128)(2,1)}, bf16[128,1408]{1,0:T(8,128)(2,1)S(1)}, u32[]{:S(2)}) copy-start(bf16[128,1408]{1,0:T(8,128)(2,1)S(1)} %gather_fusion.5) | copy-start | bytes 1081348
  230.9 21.0 %collective-permute-start.2 = (bf16[128,704]{0,1:T(8,128)(2,1)S(1)}, bf16[128,704]{0,1:T(8,128)(2,1)S(1)}, u32[]{:S(2)}, u32[]{:S(2)}) collective-permute-start(bf16[128,704]{0,1:T(8,128)(2,1)S(1)} %collective-permute-done.1), channel_id=1, source_target_pairs={{0,8},{4,12},{8,0},{12,4},{16,24},{20,28},{24,16},{28,20},{1,9},{5... | collective-permute-start | bytes 540680 | tf_op jit(solution)/shard_map/ppermute | solution.py:13
  250.7 8.6 %collective-permute-start = (bf16[128,704]{0,1:T(8,128)(2,1)S(1)}, bf16[128,704]{0,1:T(8,128)(2,1)S(1)}, u32[]{:S(2)}, u32[]{:S(2)}) collective-permute-start(bf16[128,704]{0,1:T(8,128)(2,1)S(1)} %get-tuple-element.11), channel_id=1, source_target_pairs={{4,0},{8,4},{12,8},{16,12},{20,16},{24,20},{28,24},{5,1},{9,5},{13... | collective-permute-start | bytes 540680 | tf_op jit(solution)/shard_map/ppermute | solution.py:19
  252.0 14.2 %collective-permute-start.3 = (bf16[128,704]{0,1:T(8,128)(2,1)S(1)}, bf16[128,704]{0,1:T(8,128)(2,1)S(1)}, u32[]{:S(2)}, u32[]{:S(2)}) collective-permute-start(bf16[128,704]{0,1:T(8,128)(2,1)S(1)} %collective-permute-done.2), channel_id=1, source_target_pairs={{0,16},{4,20},{8,24},{12,28},{16,0},{20,4},{24,8},{28,12},{1,17},{... | collective-permute-start | bytes 540680 | tf_op jit(solution)/shard_map/ppermute | solution.py:13
  280.0 103.7 %all-reduce.9.cloned.1.call-start = ((), (), s32[]{:S(2)}) async-start(), calls=%async_computation.9 | async-start | bytes 1441792 | tf_op jit(solution)/shard_map/psum | solution.py:81
  317.1 1.5 collective-permute-start.5
  318.6 6.6 %collective-permute-start.6 = (bf16[128,704]{0,1:T(8,128)(2,1)S(1)}, bf16[128,704]{0,1:T(8,128)(2,1)S(1)}, u32[]{:S(2)}, u32[]{:S(2)}) collective-permute-start(bf16[128,704]{0,1:T(8,128)(2,1)S(1)} %collective-permute-done.5), channel_id=1, source_target_pairs={{0,8},{4,12},{8,0},{12,4},{16,24},{20,28},{24,16},{28,20},{1,9},{5... | collective-permute-start | bytes 540680 | tf_op jit(solution)/shard_map/ppermute | solution.py:13
  320.9 10.7 %copy-start.21 = (bf16[128,1408]{1,0:T(8,128)(2,1)}, bf16[128,1408]{1,0:T(8,128)(2,1)S(1)}, u32[]{:S(2)}) copy-start(bf16[128,1408]{1,0:T(8,128)(2,1)S(1)} %gather_fusion.6) | copy-start | bytes 1081348
  321.2 10.5 %collective-permute-start.4 = (bf16[128,704]{0,1:T(8,128)(2,1)S(1)}, bf16[128,704]{0,1:T(8,128)(2,1)S(1)}, u32[]{:S(2)}, u32[]{:S(2)}) collective-permute-start(bf16[128,704]{0,1:T(8,128)(2,1)S(1)} %get-tuple-element.9), channel_id=1, source_target_pairs={{4,0},{8,4},{12,8},{16,12},{20,16},{24,20},{28,24},{5,1},{9,5},{13... | collective-permute-start | bytes 540680 | tf_op jit(solution)/shard_map/ppermute | solution.py:19
  325.1 11.5 %collective-permute-start.7 = (bf16[128,704]{0,1:T(8,128)(2,1)S(1)}, bf16[128,704]{0,1:T(8,128)(2,1)S(1)}, u32[]{:S(2)}, u32[]{:S(2)}) collective-permute-start(bf16[128,704]{0,1:T(8,128)(2,1)S(1)} %collective-permute-done.6), channel_id=1, source_target_pairs={{0,16},{4,20},{8,24},{12,28},{16,0},{20,4},{24,8},{28,12},{1,17},{... | collective-permute-start | bytes 540680 | tf_op jit(solution)/shard_map/ppermute | solution.py:13
  343.3 5.1 slice-start.4
  343.4 40.4 %copy-start.3 = (bf16[128,1408]{1,0:T(8,128)(2,1)}, bf16[128,1408]{1,0:T(8,128)(2,1)S(1)}, u32[]{:S(2)}) copy-start(bf16[128,1408]{1,0:T(8,128)(2,1)S(1)} %bitcast_select_fusion.1) | copy-start | bytes 1081348
  350.8 104.2 %all-reduce.11.cloned.1.call-start = ((), (), s32[]{:S(2)}) async-start(), calls=%async_computation.10 | async-start | bytes 1441792 | tf_op jit(solution)/shard_map/psum | solution.py:81
  388.5 1.5 collective-permute-start.9
  389.9 6.6 %collective-permute-start.10 = (bf16[128,704]{0,1:T(8,128)(2,1)S(1)}, bf16[128,704]{0,1:T(8,128)(2,1)S(1)}, u32[]{:S(2)}, u32[]{:S(2)}) collective-permute-start(bf16[128,704]{0,1:T(8,128)(2,1)S(1)} %collective-permute-done.9), channel_id=1, source_target_pairs={{0,8},{4,12},{8,0},{12,4},{16,24},{20,28},{24,16},{28,20},{1,9},{5... | collective-permute-start | bytes 540680 | tf_op jit(solution)/shard_map/ppermute | solution.py:13
  392.3 10.7 %copy-start.22 = (bf16[128,1408]{1,0:T(8,128)(2,1)}, bf16[128,1408]{1,0:T(8,128)(2,1)S(1)}, u32[]{:S(2)}) copy-start(bf16[128,1408]{1,0:T(8,128)(2,1)S(1)} %gather_fusion.7) | copy-start | bytes 1081348
  392.6 10.5 %collective-permute-start.8 = (bf16[128,704]{0,1:T(8,128)(2,1)S(1)}, bf16[128,704]{0,1:T(8,128)(2,1)S(1)}, u32[]{:S(2)}, u32[]{:S(2)}) collective-permute-start(bf16[128,704]{0,1:T(8,128)(2,1)S(1)} %get-tuple-element.7), channel_id=1, source_target_pairs={{4,0},{8,4},{12,8},{16,12},{20,16},{24,20},{28,24},{5,1},{9,5},{13... | collective-permute-start | bytes 540680 | tf_op jit(solution)/shard_map/ppermute | solution.py:19
  396.5 11.5 %collective-permute-start.11 = (bf16[128,704]{0,1:T(8,128)(2,1)S(1)}, bf16[128,704]{0,1:T(8,128)(2,1)S(1)}, u32[]{:S(2)}, u32[]{:S(2)}) collective-permute-start(bf16[128,704]{0,1:T(8,128)(2,1)S(1)} %collective-permute-done.10), channel_id=1, source_target_pairs={{0,16},{4,20},{8,24},{12,28},{16,0},{20,4},{24,8},{28,12},{1,17},{... | collective-permute-start | bytes 540680 | tf_op jit(solution)/shard_map/ppermute | solution.py:13
  414.3 5.3 slice-start.6
  422.0 92.1 %reduce-scatter.4.cloned.1.call-start = ((), (), s32[]{:S(2)}) async-start(), calls=%async_computation.11 | async-start | bytes 5947392 | tf_op jit(solution)/shard_map/reduce_scatter | solution.py:114
  462.0 110.6 %reduce-scatter.6.cloned.1.call-start = ((), (), s32[]{:S(2)}) async-start(), calls=%async_computation.12 | async-start | bytes 6488064 | tf_op jit(solution)/shard_map/reduce_scatter | solution.py:117
  469.2 162.2 %reduce-scatter.8.cloned.1.call-start = ((), (), s32[]{:S(2)}) async-start(), calls=%async_computation.13 | async-start | bytes 6488064 | tf_op jit(solution)/shard_map/reduce_scatter | solution.py:120
  475.4 156.0 %copy-start.1 = (bf16[1,128,1408]{2,1,0:T(8,128)(2,1)S(1)}, bf16[1,128,1408]{2,1,0:T(8,128)(2,1)}, u32[]{:S(2)}) copy-start(bf16[1,128,1408]{2,1,0:T(8,128)(2,1)} %param.9) | copy-start | bytes 1081348
  (28 other events, 62.0 us)
Sparse Core Ops, SparseCore 0:
  9.5 60.9 all-gather.6
  72.0 58.1 all-gather.4
  137.6 32.9 all-reduce.4
  171.9 54.1 all-gather.10
  227.5 21.6 all-gather.8
  280.2 32.1 all-reduce.6
  350.9 32.8 all-reduce.8
  422.1 32.8 all-reduce.10
  462.2 51.8 reduce-scatter.3
  516.8 55.7 reduce-scatter.5
  575.6 55.7 reduce-scatter.7
where the time goes:
time: 639 us; the launch traced here: 638 us
  waiting for transfers between devices  479 us (75%)
  matrix products  72.9 us (11%)
  blocking collectives  26.9 us (4%)
  local copies, waits for them, and re-layouts  21 us (3%)
  starting transfers between devices  17.4 us (3%)
  between operations  14.5 us (2%)
    psum x4, waiting for transfers between devices, body(): back_mixed = upstream.astype(jnp.float32) + lax.psum(partial_back, 'tensor')  120 us
    reduce_scatter x1, waiting for transfers between devices, body(): lax.psum_scatter(down_total[None].astype(jnp.bfloat16), 'replica', scatte...  58.7 us
    reduce_scatter x1, waiting for transfers between devices, body(): lax.psum_scatter(up_total[None].astype(jnp.bfloat16), 'replica', scatter_...  58.5 us
    all_gather x1, waiting for transfers between devices, body(): lax.all_gather(w_down, 'replica', axis=1, tiled=True)  55.8 us
    all_gather x1, waiting for transfers between devices, body(): lax.all_gather(w_proj, 'replica', axis=2, tiled=True)  54.4 us
    all_gather x1, waiting for transfers between devices, body(): lax.all_gather(w_up, 'replica', axis=2, tiled=True)  52.6 us
    reduce_scatter x1, waiting for transfers between devices, body(): lax.psum_scatter(proj_total[None].astype(jnp.bfloat16), 'replica', scatte...  34.5 us
    ppermute x9, waiting for transfers between devices, from_partner(): return lax.ppermute(value, axis, pairs)  25.6 us
  transfers between devices with their start and end apart: 23, of which 19 were waited for; matrix products, arithmetic and copies ran while one was open for 8% of the time, Pallas kernels for 0%

commit v1 on v0

--- a/solution.py
+++ b/solution.py
@@ -78,7 +78,9 @@
         partial_back = jnp.einsum(
             "mf,df->md", back_hidden, up_local, preferred_element_type=jnp.float32
         )
-        back_mixed = upstream.astype(jnp.float32) + lax.psum(partial_back, "tensor")
+        back_mixed = upstream.astype(jnp.float32) + jnp.sum(
+            lax.all_gather(partial_back, "tensor"), axis=0
+        )
         mixed_grad = back_mixed.astype(jnp.bfloat16)
         input_grad = jnp.einsum(
             "mj,kij->mki", mixed_grad, proj_local, preferred_element_type=jnp.float32

time: 639 us -> 588 us (0.920)
  waiting for transfers between devices: 479 us -> 429 us
  other arithmetic: 6.25 us -> 12.8 us
    psum x4 -> x0, waiting for transfers between devices: 120 us -> none  [body(): back_mixed = upstream.astype(jnp.float32) + lax.psum(partial_back, 'tensor')]
    all_gather x0 -> x4, waiting for transfers between devices: none -> 76.8 us  [body(): lax.all_gather(partial_back, 'tensor')]
    reduce_scatter x1, waiting for transfers between devices: 34.5 us -> 54.8 us  [body(): lax.psum_scatter(proj_total[None].astype(jnp.bfloat16), 'replica', scatte...]
    all_gather x1, waiting for transfers between devices: 16.7 us -> 0.01 us  [body(): lax.all_gather(loss_grads, 'tensor', axis=2, tiled=True)]
    reduce_scatter x1, waiting for transfers between devices: 58.5 us -> 46.5 us  [body(): lax.psum_scatter(up_total[None].astype(jnp.bfloat16), 'replica', scatter_...]
  transfers between devices with their start and end apart: 23 -> 23, of which waited for: 19 -> 19; matrix products, arithmetic and copies ran while one was open for 8% -> 10% of each run, Pallas kernels for 0% -> 0%
where the time goes in v1:
time: 588 us
  waiting for transfers between devices  429 us (73%)
  matrix products  69.4 us (12%)
  blocking collectives  27 us (5%)
  local copies, waits for them, and re-layouts  17.8 us (3%)
  starting transfers between devices  17.1 us (3%)
  between operations  14.6 us (2%)
  other arithmetic  12.8 us (2%)
    all_gather x4, waiting for transfers between devices, body(): lax.all_gather(partial_back, 'tensor')  76.8 us
    reduce_scatter x1, waiting for transfers between devices, body(): lax.psum_scatter(down_total[None].astype(jnp.bfloat16), 'replica', scatte...  58.6 us
    all_gather x1, waiting for transfers between devices, body(): lax.all_gather(w_down, 'replica', axis=1, tiled=True)  55.8 us
    reduce_scatter x1, waiting for transfers between devices, body(): lax.psum_scatter(proj_total[None].astype(jnp.bfloat16), 'replica', scatte...  54.8 us
    all_gather x1, waiting for transfers between devices, body(): lax.all_gather(w_proj, 'replica', axis=2, tiled=True)  53.8 us
    all_gather x1, waiting for transfers between devices, body(): lax.all_gather(w_up, 'replica', axis=2, tiled=True)  52.6 us
    reduce_scatter x1, waiting for transfers between devices, body(): lax.psum_scatter(up_total[None].astype(jnp.bfloat16), 'replica', scatter_...  46.5 us
    ppermute x9, waiting for transfers between devices, from_partner(): return lax.ppermute(value, axis, pairs)  27.3 us
  transfers between devices with their start and end apart: 23, of which 19 were waited for; matrix products, arithmetic and copies ran while one was open for 10% of the time, Pallas kernels for 0%

profile of v1, /device:TPU:0, one launch (start us, length us, event | category | flops | bytes accessed | tf_op | source)
XLA Modules:
  0.0 587.5 jit_solution(4379998357766115841)
XLA Ops:
  9.7 8.2 %all_gather.48 = bf16[1,128,1408]{1,2,0:T(8,128)(2,1)S(1)} all-gather(bf16[1,128,704]{1,2,0:T(8,128)(2,1)S(1)} %copy-done.22), channel_id=1, replica_groups=mesh['section'=8,'tensor'=2,'replica'=2] {'tensor'}, dimensions={2}, use_global_device_ids=true | all-gather | bytes 540672 | tf_op jit(solution)/shard_map/all_gather | solution.py:50
  17.9 52.6 %all-gather.15.cloned.1.call-done = bf16[1,1408,1536]{2,1,0:T(8,128)(2,1)} async-done(((bf16[1,1408,768]{2,1,0:T(8,128)(2,1)}), bf16[1,1408,1536]{2,1,0:T(8,128)(2,1)}) %all-gather.15.cloned.1.call-update) | async-done | bytes 4325392 | tf_op jit(solution)/shard_map/all_gather | solution.py:43
  70.5 4.0 multiply_convert_fusion.3
  74.5 55.8 %all-gather.13.cloned.1.call-done = bf16[1,1536,1408]{2,1,0:T(8,128)(2,1)} async-done(((bf16[1,768,1408]{2,1,0:T(8,128)(2,1)}), bf16[1,1536,1408]{2,1,0:T(8,128)(2,1)}) %all-gather.13.cloned.1.call-update) | async-done | bytes 4325392 | tf_op jit(solution)/shard_map/all_gather | solution.py:44
  130.3 4.0 fusion.56
  137.9 24.6 %all-gather.21.cloned.1.call-done = f32[256,1408]{1,0:T(8,128)} async-done(((f32[128,1408]{1,0:T(8,128)}), f32[256,1408]{1,0:T(8,128)}) %all-gather.21.cloned.1.call-update) | async-done | bytes 1441808 | tf_op jit(solution)/shard_map/all_gather | solution.py:82
  164.4 53.8 %all-gather.19.cloned.1.call-done = bf16[1,2,704,1408]{3,2,1,0:T(8,128)(2,1)} async-done(((bf16[1,2,352,1408]{3,2,1,0:T(8,128)(2,1)}), bf16[1,2,704,1408]{3,2,1,0:T(8,128)(2,1)}) %all-gather.19.cloned.1.call-update) | async-done | bytes 3964944 | tf_op jit(solution)/shard_map/all_gather | solution.py:42
  218.1 3.3 fusion.100
  226.7 2.9 collective-permute-done.2
  232.0 4.1 multiply_convert_fusion.2
  236.1 4.8 collective-permute-done.3
  241.0 6.4 %all_gather.55 = bf16[128,1408]{0,1:T(8,128)(2,1)S(1)} all-gather(bf16[128,704]{0,1:T(8,128)(2,1)S(1)} %add_convert_fusion.6), channel_id=1, replica_groups=mesh['section'=8,'tensor'=2,'replica'=2] {'tensor'}, dimensions={1}, use_global_device_ids=true | all-gather | bytes 540672 | tf_op jit(solution)/shard_map/all_gather | solution.py:100
  248.6 4.3 fusion.53
  256.0 25.7 %all-gather.23.cloned.1.call-done = f32[256,1408]{1,0:T(8,128)} async-done(((f32[128,1408]{1,0:T(8,128)}), f32[256,1408]{1,0:T(8,128)}) %all-gather.23.cloned.1.call-update) | async-done | bytes 1441808 | tf_op jit(solution)/shard_map/all_gather | solution.py:82
  283.6 3.5 fusion.103
  292.8 2.4 collective-permute-done.6
  297.6 4.0 multiply_convert_fusion.1
  301.6 5.2 collective-permute-done.7
  306.9 6.2 %all_gather.58 = bf16[128,1408]{0,1:T(8,128)(2,1)S(1)} all-gather(bf16[128,704]{0,1:T(8,128)(2,1)S(1)} %add_convert_fusion.5), channel_id=1, replica_groups=mesh['section'=8,'tensor'=2,'replica'=2] {'tensor'}, dimensions={1}, use_global_device_ids=true | all-gather | bytes 540672 | tf_op jit(solution)/shard_map/all_gather | solution.py:100
  319.1 25.7 %all-gather.25.cloned.1.call-done = f32[256,1408]{1,0:T(8,128)} async-done(((f32[128,1408]{1,0:T(8,128)}), f32[256,1408]{1,0:T(8,128)}) %all-gather.25.cloned.1.call-update) | async-done | bytes 1441808 | tf_op jit(solution)/shard_map/all_gather | solution.py:82
  347.7 3.5 fusion.106
  356.6 2.6 collective-permute-done.10
  361.7 4.0 multiply_convert_fusion
  365.6 5.2 collective-permute-done.11
  370.9 6.3 %all_gather.61 = bf16[128,1408]{0,1:T(8,128)(2,1)S(1)} all-gather(bf16[128,704]{0,1:T(8,128)(2,1)S(1)} %add_convert_fusion.4), channel_id=1, replica_groups=mesh['section'=8,'tensor'=2,'replica'=2] {'tensor'}, dimensions={1}, use_global_device_ids=true | all-gather | bytes 540672 | tf_op jit(solution)/shard_map/all_gather | solution.py:100
  383.2 6.0 %fusion = bf16[1,1408,1536]{2,1,0:T(8,128)(2,1)} fusion(bf16[128,1536]{1,0:T(8,128)(2,1)} %copy-done.15, bf16[128,1536]{1,0:T(8,128)(2,1)} %copy-done.14, bf16[128,1536]{1,0:T(8,128)(2,1)S(1)} %copy-done.13, bf16[128,1536]{1,0:T(8,128)(2,1)S(1)} %copy-done.11, bf16[128,1408]{1,0:T(8,128)(2,1)} %copy-done.21, bf16[128,1408]{1,0:T(8,128)(2,1)} %copy-done.20, ...), kind=kOutput, calls=%fused_computation.10 | convolution fusion | flops 2228813824 | bytes 7340032 | tf_op jit(solution)/shard_map/md,mf->df/dot_general | solution.py:111
  390.5 5.9 fusion.1
  410.7 5.5 fusion.34
  416.3 4.8 fusion.112
  421.1 46.5 %reduce-scatter.6.cloned.1.call-done = bf16[1,1408,768]{2,1,0:T(8,128)(2,1)} async-done(((bf16[1,1408,1536]{2,1,0:T(8,128)(2,1)}), bf16[1,1408,768]{2,1,0:T(8,128)(2,1)}) %reduce-scatter.6.cloned.1.call-update) | async-done | bytes 2162704 | tf_op jit(solution)/shard_map/reduce_scatter | solution.py:119
  467.6 58.6 %reduce-scatter.8.cloned.1.call-done = bf16[1,768,1408]{2,1,0:T(8,128)(2,1)} async-done(((bf16[1,1536,1408]{2,1,0:T(8,128)(2,1)}), bf16[1,768,1408]{2,1,0:T(8,128)(2,1)}) %reduce-scatter.8.cloned.1.call-update) | async-done | bytes 2162704 | tf_op jit(solution)/shard_map/reduce_scatter | solution.py:122
  526.2 54.8 %reduce-scatter.4.cloned.1.call-done = bf16[1,2,352,1408]{3,2,1,0:T(8,128)(2,1)} async-done(((bf16[1,2,704,1408]{3,2,1,0:T(8,128)(2,1)}), bf16[1,2,352,1408]{3,2,1,0:T(8,128)(2,1)}) %reduce-scatter.4.cloned.1.call-update) | async-done | bytes 1982480 | tf_op jit(solution)/shard_map/reduce_scatter | solution.py:116
  (171 shorter events, 68.0 us)
Async XLA Ops:
  7.2 63.3 %all-gather.15.cloned.1.call-start = ((), (), s32[]{:S(2)}) async-start(), calls=%async_computation.4 | async-start | bytes 6488064 | tf_op jit(solution)/shard_map/all_gather | solution.py:43
  7.9 122.3 %all-gather.13.cloned.1.call-start = ((), (), s32[]{:S(2)}) async-start(), calls=%async_computation.3 | async-start | bytes 6488064 | tf_op jit(solution)/shard_map/all_gather | solution.py:44
  8.7 153.9 %all-gather.21.cloned.1.call-start = ((), (), s32[]{:S(2)}) async-start(), calls=%async_computation.10 | async-start | bytes 2162688 | tf_op jit(solution)/shard_map/all_gather | solution.py:82
  9.7 64.8 %copy-start.17 = (bf16[128,1408]{1,0:T(8,128)(2,1)}, bf16[128,1408]{1,0:T(8,128)(2,1)S(1)}, u32[]{:S(2)}) copy-start(bf16[128,1408]{1,0:T(8,128)(2,1)S(1)} %gather_fusion.4) | copy-start | bytes 1081348
  70.5 63.8 %slice-start = ((s8[4325376]{0:T(1024)(128)(4,1)}), s8[131072]{0:T(1024)(128)(4,1)S(1)}, s32[]{:S(2)}) async-start(s8[4325376]{0:T(1024)(128)(4,1)} %bitcast.167), calls=%async_computation.14 | async-start | bytes 262144
  136.7 81.4 %all-gather.19.cloned.1.call-start = ((), (), s32[]{:S(2)}) async-start(), calls=%async_computation.6 | async-start | bytes 5947392 | tf_op jit(solution)/shard_map/all_gather | solution.py:42
  137.3 110.1 %all-gather.17.cloned.1.call-start = ((), (), s32[]{:S(2)}) async-start(), calls=%async_computation.5 | async-start | bytes 1622016 | tf_op jit(solution)/shard_map/all_gather | solution.py:51
  137.9 143.8 %all-gather.23.cloned.1.call-start = ((), (), s32[]{:S(2)}) async-start(), calls=%async_computation.11 | async-start | bytes 2162688 | tf_op jit(solution)/shard_map/all_gather | solution.py:82
  221.5 1.5 collective-permute-start.1
  223.0 6.6 %collective-permute-start.2 = (bf16[128,704]{0,1:T(8,128)(2,1)S(1)}, bf16[128,704]{0,1:T(8,128)(2,1)S(1)}, u32[]{:S(2)}, u32[]{:S(2)}) collective-permute-start(bf16[128,704]{0,1:T(8,128)(2,1)S(1)} %collective-permute-done.1), channel_id=1, source_target_pairs={{0,8},{4,12},{8,0},{12,4},{16,24},{20,28},{24,16},{28,20},{1,9},{5... | collective-permute-start | bytes 540680 | tf_op jit(solution)/shard_map/ppermute | solution.py:13
  225.4 10.8 %copy-start.19 = (bf16[128,1408]{1,0:T(8,128)(2,1)}, bf16[128,1408]{1,0:T(8,128)(2,1)S(1)}, u32[]{:S(2)}) copy-start(bf16[128,1408]{1,0:T(8,128)(2,1)S(1)} %gather_fusion.5) | copy-start | bytes 1081348
  225.4 10.7 %collective-permute-start = (bf16[128,704]{0,1:T(8,128)(2,1)S(1)}, bf16[128,704]{0,1:T(8,128)(2,1)S(1)}, u32[]{:S(2)}, u32[]{:S(2)}) collective-permute-start(bf16[128,704]{0,1:T(8,128)(2,1)S(1)} %get-tuple-element.8), channel_id=1, source_target_pairs={{4,0},{8,4},{12,8},{16,12},{20,16},{24,20},{28,24},{5,1},{9,5},{13... | collective-permute-start | bytes 540680 | tf_op jit(solution)/shard_map/ppermute | solution.py:19
  229.6 11.3 %collective-permute-start.3 = (bf16[128,704]{0,1:T(8,128)(2,1)S(1)}, bf16[128,704]{0,1:T(8,128)(2,1)S(1)}, u32[]{:S(2)}, u32[]{:S(2)}) collective-permute-start(bf16[128,704]{0,1:T(8,128)(2,1)S(1)} %collective-permute-done.2), channel_id=1, source_target_pairs={{0,16},{4,20},{8,24},{12,28},{16,0},{20,4},{24,8},{28,12},{1,17},{... | collective-permute-start | bytes 540680 | tf_op jit(solution)/shard_map/ppermute | solution.py:13
  256.0 88.8 %all-gather.25.cloned.1.call-start = ((), (), s32[]{:S(2)}) async-start(), calls=%async_computation.12 | async-start | bytes 2162688 | tf_op jit(solution)/shard_map/all_gather | solution.py:82
  287.1 1.5 collective-permute-start.5
  288.6 6.6 %collective-permute-start.6 = (bf16[128,704]{0,1:T(8,128)(2,1)S(1)}, bf16[128,704]{0,1:T(8,128)(2,1)S(1)}, u32[]{:S(2)}, u32[]{:S(2)}) collective-permute-start(bf16[128,704]{0,1:T(8,128)(2,1)S(1)} %collective-permute-done.5), channel_id=1, source_target_pairs={{0,8},{4,12},{8,0},{12,4},{16,24},{20,28},{24,16},{28,20},{1,9},{5... | collective-permute-start | bytes 540680 | tf_op jit(solution)/shard_map/ppermute | solution.py:13
  291.0 23.2 %slice-start.8 = ((s8[4325376]{0:T(1024)(128)(4,1)}), s8[4194304]{0:T(1024)(128)(4,1)S(1)}, s32[]{:S(2)}) async-start(s8[4325376]{0:T(1024)(128)(4,1)} %bitcast.184), calls=%async_computation.22 | async-start | bytes 8388608
  291.0 23.2 %slice-start.9 = ((s8[4325376]{0:T(1024)(128)(4,1)}), s8[131072]{0:T(1024)(128)(4,1)S(1)}, s32[]{:S(2)}) async-start(s8[4325376]{0:T(1024)(128)(4,1)} %bitcast.184), calls=%async_computation.23 | async-start | bytes 262144
  291.0 10.5 %collective-permute-start.4 = (bf16[128,704]{0,1:T(8,128)(2,1)S(1)}, bf16[128,704]{0,1:T(8,128)(2,1)S(1)}, u32[]{:S(2)}, u32[]{:S(2)}) collective-permute-start(bf16[128,704]{0,1:T(8,128)(2,1)S(1)} %get-tuple-element.6), channel_id=1, source_target_pairs={{4,0},{8,4},{12,8},{16,12},{20,16},{24,20},{28,24},{5,1},{9,5},{13... | collective-permute-start | bytes 540680 | tf_op jit(solution)/shard_map/ppermute | solution.py:19
  295.2 11.6 %collective-permute-start.7 = (bf16[128,704]{0,1:T(8,128)(2,1)S(1)}, bf16[128,704]{0,1:T(8,128)(2,1)S(1)}, u32[]{:S(2)}, u32[]{:S(2)}) collective-permute-start(bf16[128,704]{0,1:T(8,128)(2,1)S(1)} %collective-permute-done.6), channel_id=1, source_target_pairs={{0,16},{4,20},{8,24},{12,28},{16,0},{20,4},{24,8},{28,12},{1,17},{... | collective-permute-start | bytes 540680 | tf_op jit(solution)/shard_map/ppermute | solution.py:13
  319.1 89.8 %all-gather.27.cloned.1.call-start = ((), (), s32[]{:S(2)}) async-start(), calls=%async_computation.13 | async-start | bytes 2162688 | tf_op jit(solution)/shard_map/all_gather | solution.py:82
  351.2 1.5 collective-permute-start.9
  352.6 6.6 %collective-permute-start.10 = (bf16[128,704]{0,1:T(8,128)(2,1)S(1)}, bf16[128,704]{0,1:T(8,128)(2,1)S(1)}, u32[]{:S(2)}, u32[]{:S(2)}) collective-permute-start(bf16[128,704]{0,1:T(8,128)(2,1)S(1)} %collective-permute-done.9), channel_id=1, source_target_pairs={{0,8},{4,12},{8,0},{12,4},{16,24},{20,28},{24,16},{28,20},{1,9},{5... | collective-permute-start | bytes 540680 | tf_op jit(solution)/shard_map/ppermute | solution.py:13
  355.1 23.2 %slice-start.10 = ((s8[4325376]{0:T(1024)(128)(4,1)}), s8[4194304]{0:T(1024)(128)(4,1)S(1)}, s32[]{:S(2)}) async-start(s8[4325376]{0:T(1024)(128)(4,1)} %bitcast.186), calls=%async_computation.24 | async-start | bytes 8388608
  355.1 23.2 %slice-start.11 = ((s8[4325376]{0:T(1024)(128)(4,1)}), s8[131072]{0:T(1024)(128)(4,1)S(1)}, s32[]{:S(2)}) async-start(s8[4325376]{0:T(1024)(128)(4,1)} %bitcast.186), calls=%async_computation.25 | async-start | bytes 262144
  355.1 10.5 %collective-permute-start.8 = (bf16[128,704]{0,1:T(8,128)(2,1)S(1)}, bf16[128,704]{0,1:T(8,128)(2,1)S(1)}, u32[]{:S(2)}, u32[]{:S(2)}) collective-permute-start(bf16[128,704]{0,1:T(8,128)(2,1)S(1)} %get-tuple-element.4), channel_id=1, source_target_pairs={{4,0},{8,4},{12,8},{16,12},{20,16},{24,20},{28,24},{5,1},{9,5},{13... | collective-permute-start | bytes 540680 | tf_op jit(solution)/shard_map/ppermute | solution.py:19
  359.2 11.6 %collective-permute-start.11 = (bf16[128,704]{0,1:T(8,128)(2,1)S(1)}, bf16[128,704]{0,1:T(8,128)(2,1)S(1)}, u32[]{:S(2)}, u32[]{:S(2)}) collective-permute-start(bf16[128,704]{0,1:T(8,128)(2,1)S(1)} %collective-permute-done.10), channel_id=1, source_target_pairs={{0,16},{4,20},{8,24},{12,28},{16,0},{20,4},{24,8},{28,12},{1,17},{... | collective-permute-start | bytes 540680 | tf_op jit(solution)/shard_map/ppermute | solution.py:13
  378.2 11.2 %copy-start.8 = (bf16[128,1408]{0,1:T(8,128)(2,1)}, bf16[128,1408]{0,1:T(8,128)(2,1)S(1)}, u32[]{:S(2)}) copy-start(bf16[128,1408]{0,1:T(8,128)(2,1)S(1)} %fusion.138) | copy-start | bytes 1081348
  383.1 84.4 %reduce-scatter.6.cloned.1.call-start = ((), (), s32[]{:S(2)}) async-start(), calls=%async_computation.8 | async-start | bytes 6488064 | tf_op jit(solution)/shard_map/reduce_scatter | solution.py:119
  389.2 137.0 %reduce-scatter.8.cloned.1.call-start = ((), (), s32[]{:S(2)}) async-start(), calls=%async_computation.9 | async-start | bytes 6488064 | tf_op jit(solution)/shard_map/reduce_scatter | solution.py:122
  396.4 184.6 %reduce-scatter.4.cloned.1.call-start = ((), (), s32[]{:S(2)}) async-start(), calls=%async_computation.7 | async-start | bytes 5947392 | tf_op jit(solution)/shard_map/reduce_scatter | solution.py:116
  416.3 164.7 %copy-start.1 = (bf16[1,128,1408]{2,1,0:T(8,128)(2,1)S(1)}, bf16[1,128,1408]{2,1,0:T(8,128)(2,1)}, u32[]{:S(2)}) copy-start(bf16[1,128,1408]{2,1,0:T(8,128)(2,1)} %param.9) | copy-start | bytes 1081348
  (29 other events, 93.6 us)
Sparse Core Ops, SparseCore 0:
  9.5 60.9 all-gather.14
  72.0 58.1 all-gather.12
  136.8 25.6 all-gather.20
  164.0 54.1 all-gather.18
  219.5 21.6 all-gather.16
  256.1 25.5 all-gather.22
  319.2 25.5 all-gather.24
  383.3 25.5 all-gather.26
  411.7 55.7 reduce-scatter.5
  470.3 55.7 reduce-scatter.7
  529.0 51.8 reduce-scatter.3
